TPU v7x, 128 devices: a whole 4x4x4 slice. The times are simulated.
128 devices in a mesh: region: 8 (over y, core), local: 16 (over z, x).
Axes of the slice: x: 4, y: 4, z: 4, core: 2. Of those that a mesh axis runs over, the one named last changes fastest.
Arguments:
- block_flags: int32 [32, 768], P(None, ('region', 'local')), may hold values 0 or 1
- trace: bfloat16 [32, 98304], P(None, ('region', 'local')), may hold values from 0.099609375 to 1
- w_region: bfloat16 [8, 12288, 12288], P('region', None, 'local'), may hold values from -0.0546875 to 0.0546875
- lr_weight: bfloat16 [8, 16, 8, 8, 128, 128], P('region', 'local'), may hold values from -0.1875 to 0.1875
- lr_source: int32 [8, 16, 8, 8], P('region', 'local'), may hold values from 0 to 5
- lr_target: int32 [8, 16, 8, 8], P('region', 'local'), may hold values from 0 to 95
- lr_count: int32 [8, 16, 8], P('region', 'local'), may hold values from 0 to 8, as said below
- g_decay: float32 [98304], P(('region', 'local')), may hold values from 0.5 to 0.97
- v_decay: float32 [98304], P(('region', 'local')), may hold values from 0.4 to 0.95
- g_start: float32 [98304], P(('region', 'local')), may hold values from -6 to 6
- v_start: float32 [98304], P(('region', 'local')), may hold values from -6 to 6
Outputs:
- membrane: float32 [32, 98304], P(None, ('region', 'local'))
- g_final: float32 [98304], P(('region', 'local'))
Inputs may be any that keep to these rules, and one draw needn't show every extreme that they name: lr_count is 0 for a region's own devices, exactly 8 from every device to the next region (d = (r + 1) % 8), and 1 to 8 otherwise.
All inputs are finite; a program needn't handle non-finite values. No bound on the sum of `block_flags` on one device may be relied on, other than what follows from the above.
Results may differ from a plain program's by a relative error of at most 0.0003.
Values may be sent and summed in bfloat16 or wider, within the bound.
A program may use at most 128 MiB of HBM per device.

v0:
```python
import jax
import jax.numpy as jnp
from jax import lax
from jax.sharding import PartitionSpec as P


def local(
    block_flags,
    trace,
    w_region,
    lr_weight,
    lr_source,
    lr_target,
    lr_count,
    g_decay,
    v_decay,
    g_start,
    v_start,
):
    steps = trace.shape[0]
    own_blocks = block_flags.shape[1]
    width = trace.shape[1] // own_blocks
    drive = (
        trace.reshape(steps, own_blocks, width) * block_flags[:, :, None].astype(jnp.bfloat16)
    ).reshape(steps, own_blocks * width)
    weights = w_region[0]
    rows = weights
    inner = jnp.dot(
        lax.all_gather(drive, "local", axis=1, tiled=True), rows, preferred_element_type=jnp.float32
    )
    counts = lr_count[0, 0]
    targets = lr_target[0, 0]
    sources = lr_source[0, 0]
    tiles = lr_weight[0, 0]
    regions = targets.shape[0]
    slots = targets.shape[1]
    blocks = drive.reshape(steps, own_blocks, width)
    chosen = jnp.take(blocks, sources, axis=1)
    partial_value = jnp.einsum("sdci,dcio->dcso", chosen, tiles, preferred_element_type=jnp.float32)
    live = (jnp.arange(slots, dtype=jnp.int32)[None, :] < counts[:, None]).astype(jnp.float32)
    partial_value = partial_value * live[:, :, None, None]
    arrived, arrived_ids = (
        lax.all_to_all(partial_value, "region", split_axis=0, concat_axis=0, tiled=True),
        lax.all_to_all(targets, "region", split_axis=0, concat_axis=0, tiled=True),
    )
    flat = arrived.reshape(regions * slots, steps * width)
    id_flat = arrived_ids.reshape(regions * slots)
    rows = jnp.arange(lax.axis_size("local") * own_blocks, dtype=jnp.int32)
    onehot = (id_flat[None, :] == rows[:, None]).astype(jnp.float32)
    outer = lax.psum_scatter(
        jnp.dot(onehot, flat, precision=lax.Precision.HIGHEST, preferred_element_type=jnp.float32),
        "local",
        scatter_dimension=0,
        tiled=True,
    )
    outer = (
        outer.reshape(own_blocks, steps, width)
        .transpose(1, 0, 2)
        .reshape(steps, own_blocks * width)
    )
    current = inner + outer

    def advance(carry, now):
        g_state, v_state = carry
        g_state = g_decay * g_state + (1.0 - g_decay) * now
        v_state = v_decay * v_state + (1.0 - v_decay) * g_state
        return ((g_state, v_state), v_state)

    (g_last, v_last), membrane = lax.scan(advance, (g_start, v_start), current)
    return (membrane, g_last)


def solution(mesh):
    return jax.shard_map(
        local,
        mesh=mesh,
        in_specs=(
            P(None, ("region", "local")),
            P(None, ("region", "local")),
            P("region", None, "local"),
            P("region", "local", None, None, None, None),
            P("region", "local", None, None),
            P("region", "local", None, None),
            P("region", "local", None),
            P(("region", "local")),
            P(("region", "local")),
            P(("region", "local")),
            P(("region", "local")),
        ),
        out_specs=(P(None, ("region", "local")), P(("region", "local"))),
        check_vma=False,
    )
```

profile of v0, /device:TPU:0, one launch (start us, length us, event | category | flops | bytes accessed | tf_op | source)
XLA Modules:
  0.0 195.3 jit_solution(16240093048172563462)
XLA Ops:
  7.2 4.7 %all-to-all-start = ((s32[8,1,8]{2,1,0:T(1,128)}), s32[8,1,8]{2,1,0:T(1,128)S(1)}, u32[]{:S(2)}, u32[]{:S(2)}) async-start(s32[8,1,8]{2,1,0:T(1,128)} %bitcast.50), calls=%async_computation | async-start | bytes 8192 | tf_op jit(solution)/shard_map/all_to_all | solution.py:44
  11.9 0.7 convert_element_type.12
  12.6 0.7 compare_select_fusion
  13.3 0.8 fusion.18
  14.1 0.9 bitcast_multiply_fusion.1
  15.0 0.7 gather_fusion
  15.7 1.7 fusion.4
  17.4 4.8 %all-to-all-start.1 = ((f32[8,8,32,128]{3,2,1,0:T(8,128)}), f32[8,8,32,128]{3,2,1,0:T(8,128)S(1)}, u32[]{:S(2)}, u32[]{:S(2)}) async-start(f32[8,8,32,128]{3,2,1,0:T(8,128)} %fusion.4), calls=%async_computation.1 | async-start | bytes 2097152 | tf_op jit(solution)/shard_map/all_to_all | solution.py:43
  22.7 0.7 reduce.5
  23.5 14.7 %all-to-all-done.1 = f32[8,8,32,128]{3,2,1,0:T(8,128)S(1)} async-done(((f32[8,8,32,128]{3,2,1,0:T(8,128)}), f32[8,8,32,128]{3,2,1,0:T(8,128)S(1)}, u32[]{:S(2)}, u32[]{:S(2)}) %all-to-all-start.1) | async-done | bytes 1048608 | tf_op jit(solution)/shard_map/all_to_all | solution.py:43
  38.1 2.6 %fusion.10 = f32[96,4096]{1,0:T(8,128)} fusion(f32[8,8,32,128]{3,2,1,0:T(8,128)S(1)} %all-to-all-done.1, s32[64]{0:T(128)S(1)} %eq.15), kind=kOutput, calls=%fused_computation.10 | convolution fusion | flops 301996032 | bytes 2621696 | tf_op jit(solution)/shard_map/dot_general | solution.py:51
  42.3 28.0 %all_gather.3 = bf16[32,12288]{1,0:T(8,128)(2,1)S(1)} all-gather(bf16[32,768]{1,0:T(8,128)(2,1)S(1)} %bitcast_multiply_fusion), channel_id=1, replica_groups=mesh['region'=8,'local'=16] {'local'}, dimensions={1}, use_global_device_ids=true | all-gather | bytes 835584 | tf_op jit(solution)/shard_map/all_gather | solution.py:29
  70.2 61.4 %all-reduce.3.cloned.1.call-done = f32[96,4096]{1,0:T(8,128)} async-done(((f32[96,4096]{1,0:T(8,128)}), f32[96,4096]{1,0:T(8,128)}) %all-reduce.3.cloned.1.call-update) | async-done | bytes 1572880
  131.7 1.0 constant_dynamic-slice_fusion
  132.7 9.6 %fusion.7 = f32[32,768]{1,0:T(8,128)S(1)} fusion(bf16[32,12288]{1,0:T(8,128)(2,1)S(1)} %all_gather.3, bf16[1,12288,768]{2,1,0:T(8,128)(2,1)} %param.15, f32[4,8,6,128]{3,2,1,0:T(8,128)S(1)} %bitcast.48), kind=kOutput, calls=%fused_computation.9 | convolution fusion | flops 604004352 | bytes 19857408 | tf_op jit(solution)/shard_map/dot_general | solution.py:28
  142.4 45.5 %while.14 = (s32[]{:T(128)}, f32[768]{0:T(1024)S(1)}, f32[768]{0:T(1024)S(1)}, f32[32,768]{1,0:T(8,128)}, f32[768]{0:T(1024)S(1)}, /*index=5*/f32[32,768]{1,0:T(8,128)S(1)}, f32[768]{0:T(1024)S(1)}, s32[]{:T(128)}, s32[]{:T(128)}) while((s32[]{:T(128)}, f32[768]{0:T(1024)S(1)}, f32[768]{0:T(1024)S(1)}, f32[32,768]{1,0:T(8,128)}, ...), condition=%wide.region_2.3_spmd, body=%wide.region_1.2_spmd.sunk | while | flops 6146 | bytes 40037 | solution.py:69
  142.4 1.4 dynamic_update_slice.5
  143.9 1.4 dynamic_update_slice.5
  145.3 1.4 dynamic_update_slice.5
  146.7 1.4 dynamic_update_slice.5
  148.1 1.4 dynamic_update_slice.5
  149.5 1.4 dynamic_update_slice.5
  151.0 1.4 dynamic_update_slice.5
  152.4 1.4 dynamic_update_slice.5
  153.8 1.4 dynamic_update_slice.5
  155.2 1.4 dynamic_update_slice.5
  156.7 1.4 dynamic_update_slice.5
  158.1 1.4 dynamic_update_slice.5
  159.5 1.4 dynamic_update_slice.5
  160.9 1.4 dynamic_update_slice.5
  162.3 1.4 dynamic_update_slice.5
  163.8 1.4 dynamic_update_slice.5
  165.2 1.4 dynamic_update_slice.5
  166.6 1.4 dynamic_update_slice.5
  168.0 1.4 dynamic_update_slice.5
  169.5 1.4 dynamic_update_slice.5
  170.9 1.4 dynamic_update_slice.5
  172.3 1.4 dynamic_update_slice.5
  173.7 1.4 dynamic_update_slice.5
  175.1 1.4 dynamic_update_slice.5
  176.6 1.4 dynamic_update_slice.5
  178.0 1.4 dynamic_update_slice.5
  179.4 1.4 dynamic_update_slice.5
  180.8 1.4 dynamic_update_slice.5
  182.3 1.4 dynamic_update_slice.5
  183.7 1.4 dynamic_update_slice.5
  185.1 1.4 dynamic_update_slice.5
  186.5 1.4 dynamic_update_slice.5
  (124 shorter events, 3.3 us)
Async XLA Ops:
  7.2 8.5 %copy-start = (bf16[1,1,8,8,128,128]{5,4,3,2,1,0:T(8,128)(2,1)S(1)}, bf16[1,1,8,8,128,128]{5,4,3,2,1,0:T(8,128)(2,1)}, u32[]{:S(2)}) copy-start(bf16[1,1,8,8,128,128]{5,4,3,2,1,0:T(8,128)(2,1)} %param.16) | copy-start | bytes 6291460
  7.2 10.2 %all-to-all-start = ((s32[8,1,8]{2,1,0:T(1,128)}), s32[8,1,8]{2,1,0:T(1,128)S(1)}, u32[]{:S(2)}, u32[]{:S(2)}) async-start(s32[8,1,8]{2,1,0:T(1,128)} %bitcast.50), calls=%async_computation | async-start | bytes 8192 | tf_op jit(solution)/shard_map/all_to_all | solution.py:44
  17.4 20.8 %all-to-all-start.1 = ((f32[8,8,32,128]{3,2,1,0:T(8,128)}), f32[8,8,32,128]{3,2,1,0:T(8,128)S(1)}, u32[]{:S(2)}, u32[]{:S(2)}) async-start(f32[8,8,32,128]{3,2,1,0:T(8,128)} %fusion.4), calls=%async_computation.1 | async-start | bytes 2097152 | tf_op jit(solution)/shard_map/all_to_all | solution.py:43
  22.2 109.5 %all-reduce.3.cloned.1.call-start = ((), (), s32[]{:S(2)}) async-start(), calls=%async_computation.2 | async-start | bytes 3145728
  23.5 17.4 %copy-start.7 = (u32[128]{0:T(128)S(1)}, u32[128]{0:T(128)}, u32[]{:S(2)}) copy-start(u32[128]{0:T(128)} %constant.38) | copy-start | bytes 1540
  23.5 18.8 %copy-start.2 = (bf16[32,768]{1,0:T(8,128)(2,1)S(1)}, bf16[32,768]{1,0:T(8,128)(2,1)}, u32[]{:S(2)}) copy-start(bf16[32,768]{1,0:T(8,128)(2,1)} %param.14) | copy-start | bytes 147460
  132.6 9.7 %copy-start.1 = (f32[768]{0:T(1024)S(1)}, f32[768]{0:T(1024)}, u32[]{:S(2)}) copy-start(f32[768]{0:T(1024)} %param.23) | copy-start | bytes 9220
  132.6 9.7 %copy-start.4 = (f32[768]{0:T(1024)S(1)}, f32[768]{0:T(1024)}, u32[]{:S(2)}) copy-start(f32[768]{0:T(1024)} %param.22) | copy-start | bytes 9220
  132.7 9.7 %copy-start.5 = (f32[768]{0:T(1024)S(1)}, f32[768]{0:T(1024)}, u32[]{:S(2)}) copy-start(f32[768]{0:T(1024)} %param.20) | copy-start | bytes 9220
  132.7 9.7 %copy-start.6 = (f32[768]{0:T(1024)S(1)}, f32[768]{0:T(1024)}, u32[]{:S(2)}) copy-start(f32[768]{0:T(1024)} %param.21) | copy-start | bytes 9220
  187.9 0.6 copy-start.3
Sparse Core Ops, SparseCore 0:
  40.9 90.7 all-reduce.2
where the time goes:
time: 198 us; the launch traced here: 195 us
  waiting for transfers between devices  76.1 us (38%)
  local copies, waits for them, and re-layouts  48.4 us (24%)
  blocking collectives  28 us (14%)
  between operations  14.8 us (7%)
  matrix products  13.9 us (7%)
  starting transfers between devices  9.54 us (5%)
  other arithmetic  4.04 us (2%)
    unnamed x2, waiting for transfers between devices  61.4 us
    dynamic_update_slice x32, local copies, waits for them, and re-layouts, local(): (g_last, v_last), membrane = lax.scan(advance, (g_start, v_start), current)  43.8 us
    all_gather x1, blocking collectives, local(): lax.all_gather(drive, 'local', axis=1, tiled=True)  28 us
    all_to_all x1, waiting for transfers between devices, local(): lax.all_to_all(partial_value, 'region', split_axis=0, concat_axis=0, tile...  14.7 us
    dot_general x1, matrix products, local(): jnp.dot(lax.all_gather(drive, 'local', axis=1, tiled=True), rows, preferr...  9.64 us
    all_to_all x1, starting transfers between devices, local(): lax.all_to_all(partial_value, 'region', split_axis=0, concat_axis=0, tile...  4.8 us
    all_to_all x1, starting transfers between devices, local(): lax.all_to_all(targets, 'region', split_axis=0, concat_axis=0, tiled=True)  4.7 us
  transfers between devices with their start and end apart: 3, of which 2 were waited for; matrix products, arithmetic and copies ran while one was open for 4% of the time, Pallas kernels for 0%

commit v1 on v0

v1 whole, which is shorter than its diff:
```python
import jax
import jax.numpy as jnp
from jax import lax
from jax.experimental import pallas as pl
from jax.experimental.pallas import tpu as pltpu
from jax.sharding import PartitionSpec as P

MESH = pl.DeviceIdType.MESH
T, B, NB = 32, 128, 6
R, L, Q, CAP = 8, 16, 4, 8
CH = T // Q
ORDER = (4, 3, 5, 2, 6, 1, 7)
LEVELS = 32767.0


def kernel(
    flags, trace, src, cnt, tgt, gd, vd, g0, v0, w_hbm, lrw_hbm,
    out, gfin,
    wv, lrw, dbuf, dblk, idrow, stage, send1, recv1, msend, mrecv,
    send2, recv2, acc, rows,
    wsem, lsem, ag_s, ag_r, d_s, d_r, m_s, m_r, o_s, o_r, own_sem,
):
    r, l = lax.axis_index("region"), lax.axis_index("local")
    z, x = l // Q, l % Q

    barrier = pltpu.get_barrier_semaphore()
    for k in ORDER:
        for i in range(Q):
            pl.semaphore_signal(
                barrier, inc=1, device_id=((r + k) % R, z * Q + i), device_id_type=MESH
            )
    for i in range(1, L):
        pl.semaphore_signal(barrier, inc=1, device_id=(r, (l + i) % L), device_id_type=MESH)

    def lr_copy(n):
        return pltpu.make_async_copy(
            lrw_hbm.at[(r + ORDER[n]) % R], lrw.at[n], lsem.at[n]
        )

    def w_copy(i):
        return pltpu.make_async_copy(
            w_hbm.at[pl.ds(i * (NB * B), NB * B)], wv.at[i], wsem.at[i]
        )

    for n in range(R - 1):
        lr_copy(n).start()
    for dz in range(Q):
        for dx in range(Q):
            w_copy((z + dz) % Q * Q + (x + dx) % Q).start()

    flag_t = flags[...].astype(jnp.float32).T
    for b in range(NB):
        cols = slice(b * B, (b + 1) * B)
        d = (trace[:, cols].astype(jnp.float32) * flag_t[:, b : b + 1]).astype(jnp.bfloat16)
        dblk[b] = d
        dbuf[l, :, cols] = d

    lane = lax.broadcasted_iota(jnp.int32, (R, B), 1)
    idrow[...] = jnp.zeros((R, B), jnp.int32)
    t = tgt[...]
    owner = (t * 43) // 256
    idrow[:, 0:CAP] = owner * 8 + (t - owner * NB) + 1
    ids = pltpu.roll(idrow[...], x * CAP, 1)
    idrow[...] = ids

    pl.semaphore_wait(barrier, (R - 1) * Q + L - 1)

    def ag_copy(block, peer, sem):
        return pltpu.make_async_remote_copy(
            src_ref=dbuf.at[block],
            dst_ref=dbuf.at[block],
            send_sem=ag_s.at[sem],
            recv_sem=ag_r.at[block],
            device_id=(r, peer),
            device_id_type=MESH,
        )

    sent = []

    def go(c):
        c.start()
        sent.append(c)

    for dx in range(1, Q):
        go(ag_copy(l, z * Q + (x + dx) % Q, dx))

    row1 = lax.broadcasted_iota(jnp.int32, (1, B), 1)
    for n, k in enumerate(ORDER):
        d = (r + k) % R
        lr_copy(n).wait()
        st = stage.at[n % 2]
        for j in range(CAP):
            p = jnp.dot(dblk[src[d, j]], lrw[n, j], preferred_element_type=jnp.float32)
            st[pl.ds(j, T, stride=CAP), :] = p
        tiles = st[...].reshape(T, CAP, B)
        peak = jnp.max(jnp.max(jnp.abs(tiles), axis=0), axis=0, keepdims=True)
        factor = LEVELS / jnp.maximum(peak, 1e-30)
        send1[k - 1] = jnp.round(tiles * factor[None]).astype(jnp.int16)
        base = ((k - 1) % Q) * (Q * CAP)
        alive = (row1 - x * CAP) < cnt[0, d]
        row = jnp.where(alive, idrow[pl.ds(d, 1), :], 0)
        msend[k - 1, 0:1, :] = pltpu.roll(row, base, 1).astype(jnp.float32)
        msend[k - 1, 1:2, :] = peak * (1.0 / LEVELS)
        for i in range(Q):
            go(
                pltpu.make_async_remote_copy(
                    src_ref=msend.at[k - 1],
                    dst_ref=mrecv.at[k - 1, x],
                    send_sem=m_s.at[k - 1, i],
                    recv_sem=m_r.at[k - 1, x],
                    device_id=(d, z * Q + i),
                    device_id_type=MESH,
                )
            )
            go(
                pltpu.make_async_remote_copy(
                    src_ref=send1.at[k - 1, pl.ds(i * CH, CH)],
                    dst_ref=recv1.at[k - 1, x],
                    send_sem=d_s.at[k - 1, i],
                    recv_sem=d_r.at[k - 1, x],
                    device_id=(d, z * Q + i),
                    device_id_type=MESH,
                )
            )

    for dx in range(Q):
        block = z * Q + (x + dx) % Q
        if dx:
            ag_copy(block, l, 0).wait_recv()
        for dz in range(1, Q):
            go(ag_copy(block, (z + dz) % Q * Q + x, 4 + dx * 3 + dz - 1))

    acc[...] = jnp.zeros_like(acc)

    def inner(dz, dx, wait):
        i = (z + dz) % Q * Q + (x + dx) % Q
        w_copy(i).wait()
        if wait:
            ag_copy(i, l, 0).wait_recv()
        acc[...] += jnp.dot(dbuf[i], wv[i], preferred_element_type=jnp.float32)

    lax.fori_loop(0, Q, lambda i, c: (inner(0, i, False), c)[1], 0)
    lax.fori_loop(Q, L, lambda i, c: (inner(i // Q, i % Q, True), c)[1], 0)

    for k in range(R - 1):
        for i in range(Q):
            pltpu.make_async_copy(mrecv.at[k, i], mrecv.at[k, i], m_r.at[k, i]).wait()
            pltpu.make_async_copy(recv1.at[k, i], recv1.at[k, i], d_r.at[k, i]).wait()

    place = lax.broadcasted_iota(jnp.int32, (B, B), 0) + 1
    parts = []
    for half, ks in ((0, range(0, 4)), (1, range(4, 7))):
        idv = jnp.zeros((1, B), jnp.float32)
        for k in ks:
            for i in range(Q):
                idv = idv + mrecv[k, i, 0:1, :]
        hot = (place == idv.astype(jnp.int32)).astype(jnp.bfloat16)
        parts.append(hot[:, : len(ks) * Q * CAP])
    hot = jnp.concatenate(parts, axis=1)
    hot2 = jnp.concatenate([hot, hot], axis=1)

    for s in range(0, CH, 2):
        his, los = [], []
        for u in range(2):
            tiles = []
            for k in range(R - 1):
                for i in range(Q):
                    q = recv1[k, i, s + u].astype(jnp.float32)
                    tiles.append(q * mrecv[k, i, 1:2, :])
            f = jnp.concatenate(tiles, axis=0)
            hi = f.astype(jnp.bfloat16)
            his.append(hi)
            los.append((f - hi.astype(jnp.float32)).astype(jnp.bfloat16))
        rhs = jnp.concatenate(
            [jnp.concatenate(his, axis=1), jnp.concatenate(los, axis=1)], axis=0
        )
        res = jnp.dot(hot2, rhs, preferred_element_type=jnp.float32)
        for u in range(2):
            for o in range(L):
                send2[o, s + u] = res[o * 8 : o * 8 + NB, u * B : (u + 1) * B]

    for i in range(1, L):
        o = (l + i) % L
        go(
            pltpu.make_async_remote_copy(
                src_ref=send2.at[o],
                dst_ref=recv2.at[z, pl.ds(x * CH, CH)],
                send_sem=o_s.at[i],
                recv_sem=o_r.at[l],
                device_id=(r, o),
                device_id_type=MESH,
            )
        )
    own = pltpu.make_async_copy(send2.at[l], recv2.at[z, pl.ds(x * CH, CH)], own_sem)
    own.start()

    for b in range(NB):
        rows[pl.ds(b, T, stride=8), :] = acc[:, b * B : (b + 1) * B]

    own.wait()
    for i in range(1, L):
        o = (l + i) % L
        dst = recv2.at[o // Q, pl.ds(o % Q * CH, CH)]
        pltpu.make_async_copy(dst, dst, o_r.at[o]).wait()

    g, v = g0[...], v0[...]
    gdec, vdec = gd[...], vd[...]
    gin, vin = 1.0 - gdec, 1.0 - vdec
    for step in range(T):
        now = rows[step * 8 : step * 8 + NB, :]
        outer = recv2[0, step] + recv2[1, step] + recv2[2, step] + recv2[3, step]
        g = gdec * g + gin * (now + outer)
        v = vdec * v + vin * g
        rows[step * 8 : step * 8 + NB, :] = v
    gfin[...] = g
    for b in range(NB):
        out[:, b * B : (b + 1) * B] = rows[pl.ds(b, T, stride=8), :]

    for c in sent:
        c.wait_send()


def local(
    block_flags, trace, w_region, lr_weight, lr_source, lr_target, lr_count,
    g_decay, v_decay, g_start, v_start,
):
    vmem = pl.BlockSpec(memory_space=pltpu.VMEM)
    smem = pl.BlockSpec(memory_space=pltpu.SMEM)
    hbm = pl.BlockSpec(memory_space=pl.ANY)
    f32, bf16, dma = jnp.float32, jnp.bfloat16, pltpu.SemaphoreType.DMA
    membrane, g_last = pl.pallas_call(
        kernel,
        out_shape=(
            jax.ShapeDtypeStruct((T, NB * B), f32),
            jax.ShapeDtypeStruct((NB, B), f32),
        ),
        in_specs=[vmem, vmem, smem, smem, vmem, vmem, vmem, vmem, vmem, hbm, hbm],
        out_specs=(vmem, vmem),
        scratch_shapes=[
            pltpu.VMEM((L, NB * B, NB * B), bf16),
            pltpu.VMEM((R - 1, CAP, B, B), bf16),
            pltpu.VMEM((L, T, NB * B), bf16),
            pltpu.VMEM((NB, T, B), bf16),
            pltpu.VMEM((R, B), jnp.int32),
            pltpu.VMEM((2, T * CAP, B), f32),
            pltpu.VMEM((R - 1, T, CAP, B), jnp.int16),
            pltpu.VMEM((R - 1, Q, CH, CAP, B), jnp.int16),
            pltpu.VMEM((R - 1, 2, B), f32),
            pltpu.VMEM((R - 1, Q, 2, B), f32),
            pltpu.VMEM((L, CH, NB, B), f32),
            pltpu.VMEM((Q, T, NB, B), f32),
            pltpu.VMEM((T, NB * B), f32),
            pltpu.VMEM((T * 8, B), f32),
            dma((L,)),
            dma((R - 1,)),
            dma((L,)),
            dma((L,)),
            dma((R - 1, Q)),
            dma((R - 1, Q)),
            dma((R - 1, Q)),
            dma((R - 1, Q)),
            dma((L,)),
            dma((L,)),
            dma(()),
        ],
        compiler_params=pltpu.CompilerParams(
            collective_id=0, has_side_effects=True, vmem_limit_bytes=60 * 2**20
        ),
        name="window",
    )(
        block_flags.T,
        trace,
        lr_source.reshape(R, CAP),
        lr_count.reshape(1, R),
        lr_target.reshape(R, CAP),
        g_decay.reshape(NB, B),
        v_decay.reshape(NB, B),
        g_start.reshape(NB, B),
        v_start.reshape(NB, B),
        w_region.reshape(L * NB * B, NB * B),
        lr_weight.reshape(R, CAP, B, B),
    )
    return membrane, g_last.reshape(NB * B)


def solution(mesh):
    return jax.shard_map(
        local,
        mesh=mesh,
        in_specs=(
            P(None, ("region", "local")),
            P(None, ("region", "local")),
            P("region", None, "local"),
            P("region", "local", None, None, None, None),
            P("region", "local", None, None),
            P("region", "local", None, None),
            P("region", "local", None),
            P(("region", "local")),
            P(("region", "local")),
            P(("region", "local")),
            P(("region", "local")),
        ),
        out_specs=(P(None, ("region", "local")), P(("region", "local"))),
        check_vma=False,
    )
```

time: 198 us -> 38.3 us (0.19); the launches traced: 195 us -> 38 us
  waiting for transfers between devices: 76.1 us -> 0 us
  local copies, waits for them, and re-layouts: 48.4 us -> 2.81 us
  Pallas kernels: 0 us -> 34.6 us
  blocking collectives: 28 us -> 0 us
  between operations: 14.8 us -> 0.64 us
  matrix products: 13.9 us -> 0 us
  starting transfers between devices: 9.54 us -> 0 us
  other arithmetic: 4.04 us -> 0 us
    unnamed x2 -> x0, waiting for transfers between devices: 61.4 us -> none
    dynamic_update_slice x32 -> x0, local copies, waits for them, and re-layouts: 43.8 us -> none  [local(): (g_last, v_last), membrane = lax.scan(advance, (g_start, v_start), current)]
    pallas_call x0 -> x1, Pallas kernels: none -> 34.6 us  [local(): pl.pallas_call(kernel, out_shape=(jax.ShapeDtypeStruct((T, NB * B), f32),...]
    all_gather x1 -> x0, blocking collectives: 28 us -> none  [local(): lax.all_gather(drive, 'local', axis=1, tiled=True)]
    all_to_all x2 -> x0, waiting for transfers between devices: 14.7 us -> none  [the longest x1 14.7 us: local(): lax.all_to_all(partial_value, 'region', split_axis=0, concat_axis=0, tile...]
    dot_general x3 -> x0, matrix products: 13.9 us -> none  [the longest x1 9.64 us: local(): jnp.dot(lax.all_gather(drive, 'local', axis=1, tiled=True), rows, preferr...]
    all_to_all x2 -> x0, starting transfers between devices: 9.5 us -> none  [the longest x1 4.8 us: local(): lax.all_to_all(partial_value, 'region', split_axis=0, concat_axis=0, tile...]
  transfers between devices with their start and end apart: 3 -> 0, of which waited for: 2 -> 0; matrix products, arithmetic and copies ran while one was open for 4% -> 0% of each run, Pallas kernels for 0% -> 0%
where the time goes in v1:
time: 38.3 us; the launch traced here: 38 us
  Pallas kernels  34.6 us (90%)
  local copies, waits for them, and re-layouts  2.81 us (7%)
  between operations  0.64 us (2%)
    pallas_call x1, Pallas kernels, local(): pl.pallas_call(kernel, out_shape=(jax.ShapeDtypeStruct((T, NB * B), f32),...  34.6 us
    unnamed x2, local copies, waits for them, and re-layouts  2.81 us

profile of v1, /device:TPU:0, one launch (start us, length us, event | category | flops | bytes accessed | tf_op | source)
XLA Modules:
  0.0 38.0 jit_solution(15544251140589178764)
XLA Ops:
  0.6 34.6 %window.1 = (f32[32,768]{1,0:T(8,128)}, f32[6,128]{1,0:T(8,128)}) custom-call(s32[6,32]{1,0:T(8,128)} %bitcast.13, bf16[32,768]{1,0:T(8,128)(2,1)} %trace.1, s32[8,8]{1,0:T(8,128)} %bitcast.14, s32[1,8]{1,0:T(1,128)} %bitcast.21, s32[8,8]{1,0:T(8,128)} %bitcast.15, f32[6,128]{1,0:T(8,128)} %bitcast.16, f32[6,128]{1,0:T(8,128)} %bitcast.17, ...), custom_call_target="tpu_custom_call" | custom-call | tf_op jit(solution)/shard_map/window/pallas_call | solution.py:231
  35.2 1.5 %copy.15 = f32[32,768]{1,0:T(8,128)} copy(f32[32,768]{1,0:T(8,128)} %get-tuple-element.8) | data formatting | bytes 196608
  36.8 1.3 %copy.16 = f32[768]{0:T(1024)} copy(f32[768]{0:T(1024)} %bitcast.20) | data formatting | bytes 6144

commit v2 on v1

v2 whole, which is shorter than its diff:
```python
import jax
import jax.numpy as jnp
from jax import lax
from jax.experimental import pallas as pl
from jax.experimental.pallas import tpu as pltpu
from jax.sharding import PartitionSpec as P

MESH = pl.DeviceIdType.MESH
T, B, NB = 32, 128, 6
R, L, Q, CAP = 8, 16, 4, 8
CH = T // Q
ORDER = (4, 3, 5, 2, 6, 1, 7)
LEVELS = 32767.0
W0, W1, W2 = 4, 8, 8
W_AT = 2
AG_FIRST = True
EARLY = 6
XORDER = (1, 3, 2)
ZORDER = (4, 12, 8, 5, 13, 9, 7, 15, 11, 6, 14, 10)
OUT_ORDER = (10, 6, 14, 9, 11, 2, 8, 5, 7, 13, 15, 1, 3, 4, 12)


def kernel(
    flags_h, trace_h, src_h, cnt_h, tgt_h, gd_h, vd_h, g0_h, v0_h, w_hbm, lrw_hbm,
    out, gfin,
    flags, trace, src, cnt, tgt, gd, vd, g0, v0,
    wv, lrw, dbuf, dblk, idrow, stage, send1, recv1, msend, mrecv,
    stage2, send2, recv2, nsend, nrecv, acc, rows,
    in_sem, wsem, lsem, ag_s, ag_r, d_s, d_r, m_s, m_r, o_s, o_r, n_s, n_r, own_sem,
):
    r, l = lax.axis_index("region"), lax.axis_index("local")
    z, x = l // Q, l % Q

    small = [
        pltpu.make_async_copy(a, b, in_sem.at[n])
        for n, (a, b) in enumerate(
            (
                (trace_h, trace), (flags_h, flags), (src_h, src), (cnt_h, cnt), (tgt_h, tgt),
                (gd_h, gd), (vd_h, vd), (g0_h, g0), (v0_h, v0),
            )
        )
    ]

    def lr_copy(n):
        return pltpu.make_async_copy(
            lrw_hbm.at[(r + ORDER[n]) % R], lrw.at[n], lsem.at[n]
        )

    def member(i):
        return (z + i // Q) % Q * Q + (x + i % Q) % Q

    def w_copy(i):
        m = member(i)
        return pltpu.make_async_copy(
            w_hbm.at[pl.ds(m * (NB * B), NB * B)], wv.at[i], wsem.at[i]
        )

    for c in small[:5]:
        c.start()
    for n in range(R - 1):
        lr_copy(n).start()
    for c in small[5:]:
        c.start()

    barrier = pltpu.get_barrier_semaphore()
    for k in ORDER:
        for i in range(Q):
            pl.semaphore_signal(
                barrier, inc=1, device_id=((r + k) % R, z * Q + i), device_id_type=MESH
            )
    for i in range(1, L):
        pl.semaphore_signal(barrier, inc=1, device_id=(r, (l + i) % L), device_id_type=MESH)

    for i in range(W0):
        w_copy(i).start()

    for c in small[:5]:
        c.wait()
    flag_t = flags[...].astype(jnp.float32).T
    for b in range(NB):
        cols = slice(b * B, (b + 1) * B)
        d = (trace[:, cols].astype(jnp.float32) * flag_t[:, b : b + 1]).astype(jnp.bfloat16)
        dblk[b] = d
        dbuf[l, :, cols] = d

    idrow[...] = jnp.zeros((R, B), jnp.int32)
    t = tgt[...]
    owner = (t * 43) // 256
    idrow[:, 0:CAP] = owner * 8 + (t - owner * NB) + 1
    ids = pltpu.roll(idrow[...], x * CAP, 1)
    idrow[...] = ids

    def ag_copy(block, peer, sem):
        return pltpu.make_async_remote_copy(
            src_ref=dbuf.at[block],
            dst_ref=dbuf.at[block],
            send_sem=ag_s.at[sem],
            recv_sem=ag_r.at[block],
            device_id=(r, peer),
            device_id_type=MESH,
        )

    sent = []

    def go(c):
        c.start()
        sent.append(c)

    def own_drive():
        for dx in (2, 1, 3):
            go(ag_copy(l, z * Q + (x + dx) % Q, dx))
        for dz in (2, 1, 3):
            go(ag_copy(l, (z + dz) % Q * Q + x, 3 + dz))

    def tiles_out(k):
        d = (r + k) % R
        for i in range(Q):
            go(
                pltpu.make_async_remote_copy(
                    src_ref=msend.at[k - 1],
                    dst_ref=mrecv.at[k - 1, x],
                    send_sem=m_s.at[k - 1, i],
                    recv_sem=m_r.at[k - 1, x],
                    device_id=(d, z * Q + i),
                    device_id_type=MESH,
                )
            )
            go(
                pltpu.make_async_remote_copy(
                    src_ref=send1.at[k - 1, pl.ds(i * CH, CH)],
                    dst_ref=recv1.at[k - 1, x],
                    send_sem=d_s.at[k - 1, i],
                    recv_sem=d_r.at[k - 1, x],
                    device_id=(d, z * Q + i),
                    device_id_type=MESH,
                )
            )

    row1 = lax.broadcasted_iota(jnp.int32, (1, B), 1)
    for n, k in enumerate(ORDER):
        d = (r + k) % R
        lr_copy(n).wait()
        st = stage.at[n % 2]
        for j in range(CAP):
            p = jnp.dot(dblk[src[d, j]], lrw[n, j], preferred_element_type=jnp.float32)
            st[pl.ds(j, T, stride=CAP), :] = p
        tiles = st[...].reshape(T, CAP, B)
        peak = jnp.max(jnp.max(jnp.abs(tiles), axis=0), axis=0, keepdims=True)
        factor = LEVELS / jnp.maximum(peak, 1e-30)
        send1[k - 1] = jnp.round(tiles * factor[None]).astype(jnp.int16)
        base = ((k - 1) % Q) * (Q * CAP)
        alive = (row1 - x * CAP) < cnt[0, d]
        row = jnp.where(alive, idrow[pl.ds(d, 1), :], 0)
        msend[k - 1, 0:1, :] = pltpu.roll(row, base, 1).astype(jnp.float32)
        msend[k - 1, 1:2, :] = peak * (1.0 / LEVELS)
        if n == W_AT:
            pl.semaphore_wait(barrier, (R - 1) * Q + L - 1)
            if AG_FIRST:
                own_drive()
            for kk in ORDER[: n + 1]:
                tiles_out(kk)
        if n > W_AT:
            tiles_out(k)
    if not AG_FIRST:
        own_drive()

    for i in range(W0, W1):
        w_copy(i).start()
    acc[...] = jnp.zeros_like(acc)

    def inner(i):
        w_copy(i).wait()
        if W2 and i + W2 < L and i + W2 >= W1:
            w_copy(i + W2).start()
        acc[...] += jnp.dot(dbuf[member(i)], wv[i], preferred_element_type=jnp.float32)

    inner(0)
    for dx in XORDER:
        block = member(dx)
        ag_copy(block, l, 0).wait_recv()
        for dz in (2, 1, 3):
            go(ag_copy(block, (z + dz) % Q * Q + x, 4 + dx * 3 + dz - 1))
        inner(dx)

    def from_z(i):
        ag_copy(member(i), l, 0).wait_recv()
        inner(i)

    for i in ZORDER[:EARLY]:
        from_z(i)

    for k in range(R - 1):
        for i in range(Q):
            pltpu.make_async_copy(mrecv.at[k, i], mrecv.at[k, i], m_r.at[k, i]).wait()
            pltpu.make_async_copy(recv1.at[k, i], recv1.at[k, i], d_r.at[k, i]).wait()

    place = lax.broadcasted_iota(jnp.int32, (B, B), 0) + 1
    parts = []
    for ks in (range(0, 4), range(4, 7)):
        idv = jnp.zeros((1, B), jnp.float32)
        for k in ks:
            for i in range(Q):
                idv = idv + mrecv[k, i, 0:1, :]
        hot = (place == idv.astype(jnp.int32)).astype(jnp.bfloat16)
        parts.append(hot[:, : len(ks) * Q * CAP])
    hot = jnp.concatenate(parts, axis=1)
    hot2 = jnp.concatenate([hot, hot], axis=1)

    for s in range(0, CH, 2):
        his, los = [], []
        for u in range(2):
            tiles = []
            for k in range(R - 1):
                for i in range(Q):
                    q = recv1[k, i, s + u].astype(jnp.float32)
                    tiles.append(q * mrecv[k, i, 1:2, :])
            f = jnp.concatenate(tiles, axis=0)
            hi = f.astype(jnp.bfloat16)
            his.append(hi)
            los.append((f - hi.astype(jnp.float32)).astype(jnp.bfloat16))
        rhs = jnp.concatenate(
            [jnp.concatenate(his, axis=1), jnp.concatenate(los, axis=1)], axis=0
        )
        res = jnp.dot(hot2, rhs, preferred_element_type=jnp.float32)
        for u in range(2):
            for o in range(L):
                stage2[pl.ds(o * 64 + s + u, 8, stride=8), :] = res[
                    o * 8 : o * 8 + 8, u * B : (u + 1) * B
                ]
    for o in range(L):
        f = stage2[o * 64 : o * 64 + NB * CH, :]
        peak = jnp.max(jnp.abs(f), axis=0, keepdims=True)
        send2[o] = jnp.round(f * (LEVELS / jnp.maximum(peak, 1e-30))).astype(jnp.int16)
        nsend[o] = peak * (1.0 / LEVELS)

    for i in OUT_ORDER:
        o = member(i)
        go(
            pltpu.make_async_remote_copy(
                src_ref=nsend.at[o],
                dst_ref=nrecv.at[l],
                send_sem=n_s.at[i],
                recv_sem=n_r.at[l],
                device_id=(r, o),
                device_id_type=MESH,
            )
        )
        go(
            pltpu.make_async_remote_copy(
                src_ref=send2.at[o],
                dst_ref=recv2.at[l],
                send_sem=o_s.at[i],
                recv_sem=o_r.at[l],
                device_id=(r, o),
                device_id_type=MESH,
            )
        )
    own = [
        pltpu.make_async_copy(send2.at[l], recv2.at[l], own_sem.at[0]),
        pltpu.make_async_copy(nsend.at[l], nrecv.at[l], own_sem.at[1]),
    ]
    for c in own:
        c.start()

    for i in ZORDER[EARLY:]:
        from_z(i)

    for c in small[5:]:
        c.wait()
    for c in own:
        c.wait()
    for i in OUT_ORDER:
        o = member(i)
        pltpu.make_async_copy(nrecv.at[o], nrecv.at[o], n_r.at[o]).wait()
        pltpu.make_async_copy(recv2.at[o], recv2.at[o], o_r.at[o]).wait()

    for c in range(Q):
        f = jnp.zeros((NB * CH, B), jnp.float32)
        for zz in range(Q):
            f = f + recv2[zz * Q + c].astype(jnp.float32) * nrecv[zz * Q + c]
        for b in range(NB):
            rows[pl.ds(c * CH * 8 + b, CH, stride=8), :] = (
                acc[c * CH : (c + 1) * CH, b * B : (b + 1) * B] + f[b * CH : (b + 1) * CH]
            )

    g, v = g0[...], v0[...]
    gdec, vdec = gd[...], vd[...]
    gin, vin = 1.0 - gdec, 1.0 - vdec
    for step in range(T):
        g = gdec * g + gin * rows[step * 8 : step * 8 + NB, :]
        v = vdec * v + vin * g
        rows[step * 8 : step * 8 + NB, :] = v
    gfin[...] = g
    for b in range(NB):
        out[:, b * B : (b + 1) * B] = rows[pl.ds(b, T, stride=8), :]

    for c in sent:
        c.wait_send()


def local(
    block_flags, trace, w_region, lr_weight, lr_source, lr_target, lr_count,
    g_decay, v_decay, g_start, v_start,
):
    vmem = pl.BlockSpec(memory_space=pltpu.VMEM)
    hbm = pl.BlockSpec(memory_space=pltpu.HBM)
    f32, bf16, i16, i32 = jnp.float32, jnp.bfloat16, jnp.int16, jnp.int32
    dma = pltpu.SemaphoreType.DMA
    membrane, g_last = pl.pallas_call(
        kernel,
        out_shape=(
            jax.ShapeDtypeStruct((T, NB * B), f32),
            jax.ShapeDtypeStruct((NB, B), f32),
        ),
        in_specs=[hbm] * 11,
        out_specs=(vmem, vmem),
        scratch_shapes=[
            pltpu.VMEM((NB, T), i32),
            pltpu.VMEM((T, NB * B), bf16),
            pltpu.SMEM((R, CAP), i32),
            pltpu.SMEM((1, R), i32),
            pltpu.VMEM((R, CAP), i32),
            pltpu.VMEM((NB, B), f32),
            pltpu.VMEM((NB, B), f32),
            pltpu.VMEM((NB, B), f32),
            pltpu.VMEM((NB, B), f32),
            pltpu.VMEM((L, NB * B, NB * B), bf16),
            pltpu.VMEM((R - 1, CAP, B, B), bf16),
            pltpu.VMEM((L, T, NB * B), bf16),
            pltpu.VMEM((NB, T, B), bf16),
            pltpu.VMEM((R, B), i32),
            pltpu.VMEM((2, T * CAP, B), f32),
            pltpu.VMEM((R - 1, T, CAP, B), i16),
            pltpu.VMEM((R - 1, Q, CH, CAP, B), i16),
            pltpu.VMEM((R - 1, 2, B), f32),
            pltpu.VMEM((R - 1, Q, 2, B), f32),
            pltpu.VMEM((L * 64, B), f32),
            pltpu.VMEM((L, NB * CH, B), i16),
            pltpu.VMEM((L, NB * CH, B), i16),
            pltpu.VMEM((L, 1, B), f32),
            pltpu.VMEM((L, 1, B), f32),
            pltpu.VMEM((T, NB * B), f32),
            pltpu.VMEM((T * 8, B), f32),
            dma((9,)),
            dma((L,)),
            dma((R - 1,)),
            dma((L,)),
            dma((L,)),
            dma((R - 1, Q)),
            dma((R - 1, Q)),
            dma((R - 1, Q)),
            dma((R - 1, Q)),
            dma((L,)),
            dma((L,)),
            dma((L,)),
            dma((L,)),
            dma((2,)),
        ],
        compiler_params=pltpu.CompilerParams(
            collective_id=0, has_side_effects=True, vmem_limit_bytes=48 * 2**20
        ),
        name="window",
    )(
        *(
            pltpu.with_memory_space_constraint(a, pltpu.HBM)
            for a in (
                block_flags.T,
                trace,
                lr_source.reshape(R, CAP),
                lr_count.reshape(1, R),
                lr_target.reshape(R, CAP),
                g_decay.reshape(NB, B),
                v_decay.reshape(NB, B),
                g_start.reshape(NB, B),
                v_start.reshape(NB, B),
                w_region.reshape(L * NB * B, NB * B),
                lr_weight.reshape(R, CAP, B, B),
            )
        )
    )
    return membrane, g_last.reshape(NB * B)


def solution(mesh):
    return jax.shard_map(
        local,
        mesh=mesh,
        in_specs=(
            P(None, ("region", "local")),
            P(None, ("region", "local")),
            P("region", None, "local"),
            P("region", "local", None, None, None, None),
            P("region", "local", None, None),
            P("region", "local", None, None),
            P("region", "local", None),
            P(("region", "local")),
            P(("region", "local")),
            P(("region", "local")),
            P(("region", "local")),
        ),
        out_specs=(P(None, ("region", "local")), P(("region", "local"))),
        check_vma=False,
    )
```

time: 38.3 us -> 29.8 us (0.78)
  Pallas kernels: 34.6 us -> 27.7 us
  local copies, waits for them, and re-layouts: 2.81 us -> 1.24 us
    pallas_call x1, Pallas kernels: 34.6 us -> 27.7 us  [local(): pl.pallas_call(kernel, out_shape=(jax.ShapeDtypeStruct((T, NB * B), f32),...]
    unnamed x2, local copies, waits for them, and re-layouts: 2.81 us -> 1.24 us
where the time goes in v2:
time: 29.8 us; the launch traced here: 29.6 us
  Pallas kernels  27.7 us (93%)
  local copies, waits for them, and re-layouts  1.24 us (4%)
  between operations  0.64 us (2%)
    pallas_call x1, Pallas kernels, local(): pl.pallas_call(kernel, out_shape=(jax.ShapeDtypeStruct((T, NB * B), f32),...  27.7 us
    unnamed x2, local copies, waits for them, and re-layouts  1.24 us

profile of v2, /device:TPU:0, one launch (start us, length us, event | category | flops | bytes accessed | tf_op | source)
XLA Modules:
  0.0 29.6 jit_solution(5194144588489964825)
XLA Ops:
  0.6 27.7 %window.1 = (f32[32,768]{1,0:T(8,128)S(1)}, f32[6,128]{1,0:T(8,128)S(1)}) custom-call(s32[6,32]{1,0:T(8,128)} %bitcast.14, bf16[32,768]{1,0:T(8,128)(2,1)} %trace_h.1, s32[8,8]{1,0:T(8,128)} %bitcast.15, s32[1,8]{1,0:T(1,128)} %bitcast.21, s32[8,8]{1,0:T(8,128)} %bitcast.16, f32[6,128]{1,0:T(8,128)} %bitcast.17, f32[6,128]{1,0:T(8,128)} %bitcast.18, ...), custom_call_target="tpu_custom_call" | custom-call | tf_op jit(solution)/shard_map/window/pallas_call | solution.py:309
  28.3 0.6 %copy.15 = f32[32,768]{1,0:T(8,128)} copy(f32[32,768]{1,0:T(8,128)S(1)} %get-tuple-element.8) | data formatting | bytes 196608
  29.0 0.6 %copy.16 = f32[768]{0:T(1024)} copy(f32[768]{0:T(1024)S(1)} %bitcast.11) | data formatting | bytes 6144

commit v3 on v2

--- a/solution.py
+++ b/solution.py
@@ -11,12 +11,19 @@
 CH = T // Q
 ORDER = (4, 3, 5, 2, 6, 1, 7)
 LEVELS = 32767.0
+HALF = NB * B // 2
 W0, W1, W2 = 4, 8, 8
 W_AT = 2
-AG_FIRST = True
-EARLY = 6
-XORDER = (1, 3, 2)
-ZORDER = (4, 12, 8, 5, 13, 9, 7, 15, 11, 6, 14, 10)
+DIAG = (5, 7, 13, 15, 6, 9, 11, 14, 10)
+FIRST = (
+    "f01", "f14", "f03", "f1c", "f02", "f18", "c00", "c10", "c01", "c14", "c03", "c1c", "c02",
+    "c18",
+)
+NEXT = (
+    "c11", "c04", "c13", "c0c", "c12", "c08",
+)
+EARLY = 4
+W_ORDER = (0, 1, 4, 3, 12, 2, 8) + DIAG
 OUT_ORDER = (10, 6, 14, 9, 11, 2, 8, 5, 7, 13, 15, 1, 3, 4, 12)
 
 
@@ -30,6 +37,8 @@
 ):
     r, l = lax.axis_index("region"), lax.axis_index("local")
     z, x = l // Q, l % Q
+    zb, xb = z - z % 2, x - x % 2
+    c = z % 2 * 2 + x % 2
 
     small = [
         pltpu.make_async_copy(a, b, in_sem.at[n])
@@ -55,85 +64,79 @@
             w_hbm.at[pl.ds(m * (NB * B), NB * B)], wv.at[i], wsem.at[i]
         )
 
-    for c in small[:5]:
-        c.start()
+    for cp in small[:5]:
+        cp.start()
     for n in range(R - 1):
         lr_copy(n).start()
-    for c in small[5:]:
-        c.start()
+    for cp in small[5:]:
+        cp.start()
 
     barrier = pltpu.get_barrier_semaphore()
+    def mate(i):
+        return (zb + i // 2) * Q + xb + i % 2
+
     for k in ORDER:
         for i in range(Q):
             pl.semaphore_signal(
-                barrier, inc=1, device_id=((r + k) % R, z * Q + i), device_id_type=MESH
+                barrier, inc=1, device_id=((r + k) % R, mate(i)), device_id_type=MESH
             )
     for i in range(1, L):
         pl.semaphore_signal(barrier, inc=1, device_id=(r, (l + i) % L), device_id_type=MESH)
 
     for i in range(W0):
-        w_copy(i).start()
-
-    for c in small[:5]:
-        c.wait()
+        w_copy(W_ORDER[i]).start()
+
+    for cp in small[:5]:
+        cp.wait()
     flag_t = flags[...].astype(jnp.float32).T
     for b in range(NB):
         cols = slice(b * B, (b + 1) * B)
         d = (trace[:, cols].astype(jnp.float32) * flag_t[:, b : b + 1]).astype(jnp.bfloat16)
         dblk[b] = d
-        dbuf[l, :, cols] = d
+        dbuf[l, b // 3, :, b % 3 * B : (b % 3 + 1) * B] = d
 
     idrow[...] = jnp.zeros((R, B), jnp.int32)
     t = tgt[...]
     owner = (t * 43) // 256
     idrow[:, 0:CAP] = owner * 8 + (t - owner * NB) + 1
-    ids = pltpu.roll(idrow[...], x * CAP, 1)
+    ids = pltpu.roll(idrow[...], c * CAP, 1)
     idrow[...] = ids
 
-    def ag_copy(block, peer, sem):
+    def ag_copy(h, block, peer):
         return pltpu.make_async_remote_copy(
-            src_ref=dbuf.at[block],
-            dst_ref=dbuf.at[block],
-            send_sem=ag_s.at[sem],
-            recv_sem=ag_r.at[block],
+            src_ref=dbuf.at[block, h],
+            dst_ref=dbuf.at[block, h],
+            send_sem=ag_s,
+            recv_sem=ag_r.at[h, block],
             device_id=(r, peer),
             device_id_type=MESH,
         )
 
-    sent = []
-
-    def go(c):
-        c.start()
-        sent.append(c)
+    def remote(src, dst, send, recv, device):
+        pltpu.make_async_remote_copy(
+            src_ref=src, dst_ref=dst, send_sem=send, recv_sem=recv,
+            device_id=device, device_id_type=MESH,
+        ).start()
+
+    def drained(ref, sem):
+        pltpu.make_async_copy(ref, ref, sem).wait()
 
     def own_drive():
-        for dx in (2, 1, 3):
-            go(ag_copy(l, z * Q + (x + dx) % Q, dx))
-        for dz in (2, 1, 3):
-            go(ag_copy(l, (z + dz) % Q * Q + x, 3 + dz))
+        for a in (1, 3, 2):
+            ag_copy(0, l, member(a)).start()
+            ag_copy(1, l, member(Q * a)).start()
+
+    def own_drive2():
+        for a in (1, 3, 2):
+            ag_copy(0, l, member(Q * a)).start()
+            ag_copy(1, l, member(a)).start()
 
     def tiles_out(k):
         d = (r + k) % R
         for i in range(Q):
-            go(
-                pltpu.make_async_remote_copy(
-                    src_ref=msend.at[k - 1],
-                    dst_ref=mrecv.at[k - 1, x],
-                    send_sem=m_s.at[k - 1, i],
-                    recv_sem=m_r.at[k - 1, x],
-                    device_id=(d, z * Q + i),
-                    device_id_type=MESH,
-                )
-            )
-            go(
-                pltpu.make_async_remote_copy(
-                    src_ref=send1.at[k - 1, pl.ds(i * CH, CH)],
-                    dst_ref=recv1.at[k - 1, x],
-                    send_sem=d_s.at[k - 1, i],
-                    recv_sem=d_r.at[k - 1, x],
-                    device_id=(d, z * Q + i),
-                    device_id_type=MESH,
-                )
+            remote(msend.at[k - 1], mrecv.at[k - 1, c], m_s, m_r, (d, mate(i)))
+            remote(
+                send1.at[k - 1, pl.ds(i * CH, CH)], recv1.at[k - 1, c], d_s, d_r, (d, mate(i))
             )
 
     row1 = lax.broadcasted_iota(jnp.int32, (1, B), 1)
@@ -149,50 +152,60 @@
         factor = LEVELS / jnp.maximum(peak, 1e-30)
         send1[k - 1] = jnp.round(tiles * factor[None]).astype(jnp.int16)
         base = ((k - 1) % Q) * (Q * CAP)
-        alive = (row1 - x * CAP) < cnt[0, d]
+        alive = (row1 - c * CAP) < cnt[0, d]
         row = jnp.where(alive, idrow[pl.ds(d, 1), :], 0)
         msend[k - 1, 0:1, :] = pltpu.roll(row, base, 1).astype(jnp.float32)
         msend[k - 1, 1:2, :] = peak * (1.0 / LEVELS)
         if n == W_AT:
             pl.semaphore_wait(barrier, (R - 1) * Q + L - 1)
-            if AG_FIRST:
-                own_drive()
-            for kk in ORDER[: n + 1]:
-                tiles_out(kk)
-        if n > W_AT:
-            tiles_out(k)
-    if not AG_FIRST:
-        own_drive()
+        if n >= W_AT:
+            for m in range(n + 1) if n == W_AT else (n,):
+                if m == 0:
+                    own_drive()
+                tiles_out(ORDER[m])
+    own_drive2()
 
     for i in range(W0, W1):
-        w_copy(i).start()
+        w_copy(W_ORDER[i]).start()
     acc[...] = jnp.zeros_like(acc)
 
-    def inner(i):
-        w_copy(i).wait()
-        if W2 and i + W2 < L and i + W2 >= W1:
-            w_copy(i + W2).start()
-        acc[...] += jnp.dot(dbuf[member(i)], wv[i], preferred_element_type=jnp.float32)
-
-    inner(0)
-    for dx in XORDER:
-        block = member(dx)
-        ag_copy(block, l, 0).wait_recv()
-        for dz in (2, 1, 3):
-            go(ag_copy(block, (z + dz) % Q * Q + x, 4 + dx * 3 + dz - 1))
-        inner(dx)
-
-    def from_z(i):
-        ag_copy(member(i), l, 0).wait_recv()
-        inner(i)
-
-    for i in ZORDER[:EARLY]:
-        from_z(i)
-
-    for k in range(R - 1):
-        for i in range(Q):
-            pltpu.make_async_copy(mrecv.at[k, i], mrecv.at[k, i], m_r.at[k, i]).wait()
-            pltpu.make_async_copy(recv1.at[k, i], recv1.at[k, i], d_r.at[k, i]).wait()
+    have, loaded = {(0, 0), (1, 0)}, set()
+
+    def arrive(h, i):
+        if (h, i) not in have:
+            have.add((h, i))
+            ag_copy(h, member(i), l).wait_recv()
+
+    def load(i):
+        if i not in loaded:
+            w_copy(i).wait()
+            n = W_ORDER.index(i) + W2
+            if W2 and W1 <= n < L:
+                w_copy(W_ORDER[n]).start()
+            loaded.add(i)
+
+    def do(steps):
+        for op in steps:
+            h, i = int(op[1]), int(op[2], 16)
+            arrive(h, i)
+            if op[0] == "f":
+                for a in (1, 3, 2):
+                    other = (z + a) % Q * Q + x if h == 0 else z * Q + (x + a) % Q
+                    ag_copy(h, member(i), other).start()
+            else:
+                load(i)
+                acc[...] += jnp.dot(
+                    dbuf[member(i), h],
+                    wv[i, pl.ds(h * HALF, HALF)],
+                    preferred_element_type=jnp.float32,
+                )
+
+    rest = NEXT + tuple(f"c{h}{i:x}" for i in DIAG for h in range(2))
+    do(FIRST)
+    do(rest[:EARLY])
+
+    drained(mrecv, m_r)
+    drained(recv1, d_r)
 
     place = lax.broadcasted_iota(jnp.int32, (B, B), 0) + 1
     parts = []
@@ -235,52 +248,37 @@
 
     for i in OUT_ORDER:
         o = member(i)
-        go(
-            pltpu.make_async_remote_copy(
-                src_ref=nsend.at[o],
-                dst_ref=nrecv.at[l],
-                send_sem=n_s.at[i],
-                recv_sem=n_r.at[l],
-                device_id=(r, o),
-                device_id_type=MESH,
-            )
-        )
-        go(
-            pltpu.make_async_remote_copy(
-                src_ref=send2.at[o],
-                dst_ref=recv2.at[l],
-                send_sem=o_s.at[i],
-                recv_sem=o_r.at[l],
-                device_id=(r, o),
-                device_id_type=MESH,
-            )
-        )
+        remote(nsend.at[o], nrecv.at[l], n_s, n_r, (r, o))
+        remote(send2.at[o], recv2.at[l], o_s, o_r, (r, o))
     own = [
         pltpu.make_async_copy(send2.at[l], recv2.at[l], own_sem.at[0]),
         pltpu.make_async_copy(nsend.at[l], nrecv.at[l], own_sem.at[1]),
     ]
-    for c in own:
-        c.start()
-
-    for i in ZORDER[EARLY:]:
-        from_z(i)
-
-    for c in small[5:]:
-        c.wait()
-    for c in own:
-        c.wait()
-    for i in OUT_ORDER:
-        o = member(i)
-        pltpu.make_async_copy(nrecv.at[o], nrecv.at[o], n_r.at[o]).wait()
-        pltpu.make_async_copy(recv2.at[o], recv2.at[o], o_r.at[o]).wait()
-
-    for c in range(Q):
+    for cp in own:
+        cp.start()
+
+    do(rest[EARLY:])
+
+    for cp in small[5:]:
+        cp.wait()
+    for cp in own:
+        cp.wait()
+    drained(send1, d_s)
+    drained(mrecv, m_s)
+    drained(dbuf.at[pl.ds(0, L - 1)], ag_s)
+    drained(send2.at[pl.ds(0, L - 1)], o_s)
+    drained(nsend.at[pl.ds(0, L - 1)], n_s)
+    drained(nrecv.at[pl.ds(0, L - 1)], n_r)
+    drained(recv2.at[pl.ds(0, L - 1)], o_r)
+
+    for q in range(Q):
         f = jnp.zeros((NB * CH, B), jnp.float32)
-        for zz in range(Q):
-            f = f + recv2[zz * Q + c].astype(jnp.float32) * nrecv[zz * Q + c]
+        for u in range(Q):
+            o = (u // 2 * 2 + q // 2) * Q + u % 2 * 2 + q % 2
+            f = f + recv2[o].astype(jnp.float32) * nrecv[o]
         for b in range(NB):
-            rows[pl.ds(c * CH * 8 + b, CH, stride=8), :] = (
-                acc[c * CH : (c + 1) * CH, b * B : (b + 1) * B] + f[b * CH : (b + 1) * CH]
+            rows[pl.ds(q * CH * 8 + b, CH, stride=8), :] = (
+                acc[q * CH : (q + 1) * CH, b * B : (b + 1) * B] + f[b * CH : (b + 1) * CH]
             )
 
     g, v = g0[...], v0[...]
@@ -293,9 +291,6 @@
     gfin[...] = g
     for b in range(NB):
         out[:, b * B : (b + 1) * B] = rows[pl.ds(b, T, stride=8), :]
-
-    for c in sent:
-        c.wait_send()
 
 
 def local(
@@ -326,7 +321,7 @@
             pltpu.VMEM((NB, B), f32),
             pltpu.VMEM((L, NB * B, NB * B), bf16),
             pltpu.VMEM((R - 1, CAP, B, B), bf16),
-            pltpu.VMEM((L, T, NB * B), bf16),
+            pltpu.VMEM((L, 2, T, HALF), bf16),
             pltpu.VMEM((NB, T, B), bf16),
             pltpu.VMEM((R, B), i32),
             pltpu.VMEM((2, T * CAP, B), f32),
@@ -344,16 +339,16 @@
             dma((9,)),
             dma((L,)),
             dma((R - 1,)),
-            dma((L,)),
-            dma((L,)),
-            dma((R - 1, Q)),
-            dma((R - 1, Q)),
-            dma((R - 1, Q)),
-            dma((R - 1, Q)),
-            dma((L,)),
-            dma((L,)),
-            dma((L,)),
-            dma((L,)),
+            dma(()),
+            dma((2, L)),
+            dma(()),
+            dma(()),
+            dma(()),
+            dma(()),
+            dma(()),
+            dma(()),
+            dma(()),
+            dma(()),
             dma((2,)),
         ],
         compiler_params=pltpu.CompilerParams(

time: 29.8 us -> 26.5 us (0.89)
  Pallas kernels: 27.7 us -> 24.5 us
    pallas_call x1, Pallas kernels: 27.7 us -> 24.5 us  [local(): pl.pallas_call(kernel, out_shape=(jax.ShapeDtypeStruct((T, NB * B), f32),...]
where the time goes in v3:
time: 26.5 us; the launch traced here: 26.4 us
  Pallas kernels  24.5 us (92%)
  local copies, waits for them, and re-layouts  1.24 us (5%)
  between operations  0.64 us (2%)
    pallas_call x1, Pallas kernels, local(): pl.pallas_call(kernel, out_shape=(jax.ShapeDtypeStruct((T, NB * B), f32),...  24.5 us
    unnamed x2, local copies, waits for them, and re-layouts  1.24 us

profile of v3, /device:TPU:0, one launch (start us, length us, event | category | flops | bytes accessed | tf_op | source)
XLA Modules:
  0.0 26.4 jit_solution(8396070378052837780)
XLA Ops:
  0.6 24.5 %window.1 = (f32[32,768]{1,0:T(8,128)S(1)}, f32[6,128]{1,0:T(8,128)S(1)}) custom-call(s32[6,32]{1,0:T(8,128)} %bitcast.14, bf16[32,768]{1,0:T(8,128)(2,1)} %trace_h.1, s32[8,8]{1,0:T(8,128)} %bitcast.15, s32[1,8]{1,0:T(1,128)} %bitcast.21, s32[8,8]{1,0:T(8,128)} %bitcast.16, f32[6,128]{1,0:T(8,128)} %bitcast.17, f32[6,128]{1,0:T(8,128)} %bitcast.18, ...), custom_call_target="tpu_custom_call" | custom-call | tf_op jit(solution)/shard_map/window/pallas_call | solution.py:304
  25.1 0.6 %copy.15 = f32[32,768]{1,0:T(8,128)} copy(f32[32,768]{1,0:T(8,128)S(1)} %get-tuple-element.8) | data formatting | bytes 196608
  25.8 0.6 %copy.16 = f32[768]{0:T(1024)} copy(f32[768]{0:T(1024)S(1)} %bitcast.11) | data formatting | bytes 6144

commit v4 on v3

--- a/solution.py
+++ b/solution.py
@@ -13,7 +13,7 @@
 LEVELS = 32767.0
 HALF = NB * B // 2
 W0, W1, W2 = 4, 8, 8
-W_AT = 2
+W_AT = 1
 DIAG = (5, 7, 13, 15, 6, 9, 11, 14, 10)
 FIRST = (
     "f01", "f14", "f03", "f1c", "f02", "f18", "c00", "c10", "c01", "c14", "c03", "c1c", "c02",
@@ -40,6 +40,18 @@
     zb, xb = z - z % 2, x - x % 2
     c = z % 2 * 2 + x % 2
 
+    barrier = pltpu.get_barrier_semaphore()
+    def mate(i):
+        return (zb + i // 2) * Q + xb + i % 2
+
+    for k in ORDER:
+        for i in range(Q):
+            pl.semaphore_signal(
+                barrier, inc=1, device_id=((r + k) % R, mate(i)), device_id_type=MESH
+            )
+    for i in range(1, L):
+        pl.semaphore_signal(barrier, inc=1, device_id=(r, (l + i) % L), device_id_type=MESH)
+
     small = [
         pltpu.make_async_copy(a, b, in_sem.at[n])
         for n, (a, b) in enumerate(
@@ -70,18 +82,6 @@
         lr_copy(n).start()
     for cp in small[5:]:
         cp.start()
-
-    barrier = pltpu.get_barrier_semaphore()
-    def mate(i):
-        return (zb + i // 2) * Q + xb + i % 2
-
-    for k in ORDER:
-        for i in range(Q):
-            pl.semaphore_signal(
-                barrier, inc=1, device_id=((r + k) % R, mate(i)), device_id_type=MESH
-            )
-    for i in range(1, L):
-        pl.semaphore_signal(barrier, inc=1, device_id=(r, (l + i) % L), device_id_type=MESH)
 
     for i in range(W0):
         w_copy(W_ORDER[i]).start()
@@ -291,6 +291,17 @@
     gfin[...] = g
     for b in range(NB):
         out[:, b * B : (b + 1) * B] = rows[pl.ds(b, T, stride=8), :]
+
+
+def place(m_ref, g_ref, out, gfin, sem):
+    copies = [
+        pltpu.make_async_copy(m_ref, out, sem.at[0]),
+        pltpu.make_async_copy(g_ref, gfin, sem.at[1]),
+    ]
+    for cp in copies:
+        cp.start()
+    for cp in copies:
+        cp.wait()
 
 
 def local(
@@ -373,6 +384,18 @@
             )
         )
     )
+    membrane, g_last = pl.pallas_call(
+        place,
+        out_shape=(
+            jax.ShapeDtypeStruct((T, NB * B), f32),
+            jax.ShapeDtypeStruct((NB, B), f32),
+        ),
+        in_specs=[vmem, vmem],
+        out_specs=(hbm, hbm),
+        scratch_shapes=[dma((2,))],
+        compiler_params=pltpu.CompilerParams(vmem_limit_bytes=2**20),
+        name="place",
+    )(membrane, g_last)
     return membrane, g_last.reshape(NB * B)
 
 

time: 26.5 us -> 25.9 us (0.977)
  local copies, waits for them, and re-layouts: 1.24 us -> 0 us
  Pallas kernels: 24.5 us -> 25.1 us
    unnamed x2 -> x0, local copies, waits for them, and re-layouts: 1.24 us -> none
    pallas_call x0 -> x1, Pallas kernels: none -> 0.66 us  [local(): pl.pallas_call(place, out_shape=(jax.ShapeDtypeStruct((T, NB * B), f32),...]
where the time goes in v4:
time: 25.9 us; the launch traced here: 25.7 us
  Pallas kernels  25.1 us (97%)
  between operations  0.64 us (2%)
    pallas_call x1, Pallas kernels, local(): pl.pallas_call(kernel, out_shape=(jax.ShapeDtypeStruct((T, NB * B), f32),...  24.4 us
    pallas_call x1, Pallas kernels, local(): pl.pallas_call(place, out_shape=(jax.ShapeDtypeStruct((T, NB * B), f32),...  0.66 us

profile of v4, /device:TPU:0, one launch (start us, length us, event | category | flops | bytes accessed | tf_op | source)
XLA Modules:
  0.0 25.7 jit_solution(16859379525218861399)
XLA Ops:
  0.6 24.4 %window.1 = (f32[32,768]{1,0:T(8,128)S(1)}, f32[6,128]{1,0:T(8,128)S(1)}) custom-call(s32[6,32]{1,0:T(8,128)} %bitcast.13, bf16[32,768]{1,0:T(8,128)(2,1)} %trace_h.1, s32[8,8]{1,0:T(8,128)} %bitcast.14, s32[1,8]{1,0:T(1,128)} %bitcast.20, s32[8,8]{1,0:T(8,128)} %bitcast.15, f32[6,128]{1,0:T(8,128)} %bitcast.16, f32[6,128]{1,0:T(8,128)} %bitcast.17, ...), custom_call_target="tpu_custom_call" | custom-call | tf_op jit(solution)/shard_map/window/pallas_call | solution.py:315
  25.1 0.7 %place.1 = (f32[32,768]{1,0:T(8,128)}, f32[6,128]{1,0:T(8,128)}) custom-call(f32[32,768]{1,0:T(8,128)S(1)} %get-tuple-element.6.m_ref, f32[6,128]{1,0:T(8,128)S(1)} %get-tuple-element.7.g_ref), custom_call_target="tpu_custom_call" | custom-call | tf_op jit(solution)/shard_map/place/pallas_call | solution.py:387

commit v5 on v4

--- a/solution.py
+++ b/solution.py
@@ -12,7 +12,7 @@
 ORDER = (4, 3, 5, 2, 6, 1, 7)
 LEVELS = 32767.0
 HALF = NB * B // 2
-W0, W1, W2 = 4, 8, 8
+W0, W1, W2 = 3, 8, 8
 W_AT = 1
 DIAG = (5, 7, 13, 15, 6, 9, 11, 14, 10)
 FIRST = (
@@ -134,10 +134,10 @@
     def tiles_out(k):
         d = (r + k) % R
         for i in range(Q):
-            remote(msend.at[k - 1], mrecv.at[k - 1, c], m_s, m_r, (d, mate(i)))
             remote(
                 send1.at[k - 1, pl.ds(i * CH, CH)], recv1.at[k - 1, c], d_s, d_r, (d, mate(i))
             )
+            remote(msend.at[k - 1], mrecv.at[k - 1, c], m_s, m_r, (d, mate(i)))
 
     row1 = lax.broadcasted_iota(jnp.int32, (1, B), 1)
     for n, k in enumerate(ORDER):
@@ -205,7 +205,6 @@
     do(rest[:EARLY])
 
     drained(mrecv, m_r)
-    drained(recv1, d_r)
 
     place = lax.broadcasted_iota(jnp.int32, (B, B), 0) + 1
     parts = []
@@ -219,6 +218,7 @@
     hot = jnp.concatenate(parts, axis=1)
     hot2 = jnp.concatenate([hot, hot], axis=1)
 
+    drained(recv1, d_r)
     for s in range(0, CH, 2):
         his, los = [], []
         for u in range(2):
@@ -248,8 +248,8 @@
 
     for i in OUT_ORDER:
         o = member(i)
+        remote(send2.at[o], recv2.at[l], o_s, o_r, (r, o))
         remote(nsend.at[o], nrecv.at[l], n_s, n_r, (r, o))
-        remote(send2.at[o], recv2.at[l], o_s, o_r, (r, o))
     own = [
         pltpu.make_async_copy(send2.at[l], recv2.at[l], own_sem.at[0]),
         pltpu.make_async_copy(nsend.at[l], nrecv.at[l], own_sem.at[1]),

time: 25.9 us -> 26 us (level)
  no operation moved by 1% of the time
where the time goes in v5:
time: 26 us; the launch traced here: 25.9 us
  Pallas kernels  25.3 us (97%)
  between operations  0.64 us (2%)
    pallas_call x1, Pallas kernels, local(): pl.pallas_call(kernel, out_shape=(jax.ShapeDtypeStruct((T, NB * B), f32),...  24.6 us
    pallas_call x1, Pallas kernels, local(): pl.pallas_call(place, out_shape=(jax.ShapeDtypeStruct((T, NB * B), f32),...  0.66 us

profile of v5, /device:TPU:0, one launch (start us, length us, event | category | flops | bytes accessed | tf_op | source)
XLA Modules:
  0.0 25.9 jit_solution(7272553774179339133)
XLA Ops:
  0.6 24.6 %window.1 = (f32[32,768]{1,0:T(8,128)S(1)}, f32[6,128]{1,0:T(8,128)S(1)}) custom-call(s32[6,32]{1,0:T(8,128)} %bitcast.13, bf16[32,768]{1,0:T(8,128)(2,1)} %trace_h.1, s32[8,8]{1,0:T(8,128)} %bitcast.14, s32[1,8]{1,0:T(1,128)} %bitcast.20, s32[8,8]{1,0:T(8,128)} %bitcast.15, f32[6,128]{1,0:T(8,128)} %bitcast.16, f32[6,128]{1,0:T(8,128)} %bitcast.17, ...), custom_call_target="tpu_custom_call" | custom-call | tf_op jit(solution)/shard_map/window/pallas_call | solution.py:315
  25.2 0.7 %place.1 = (f32[32,768]{1,0:T(8,128)}, f32[6,128]{1,0:T(8,128)}) custom-call(f32[32,768]{1,0:T(8,128)S(1)} %get-tuple-element.6.m_ref, f32[6,128]{1,0:T(8,128)S(1)} %get-tuple-element.7.g_ref), custom_call_target="tpu_custom_call" | custom-call | tf_op jit(solution)/shard_map/place/pallas_call | solution.py:387
